TPU v7x, 32 devices: a whole 2x2x4 slice. The times are simulated.
32 devices in a mesh: groups: 2 (over x), seq: 16 (over z, y, core).
Axes of the slice: x: 2, y: 2, z: 4, core: 2. Of those that a mesh axis runs over, the one named last changes fastest.
Arguments:
- queries: bfloat16 [32, 32, 1024], P('seq', 'groups'), parts along dimension 1, may hold values from -1100 to 1100
- keys: bfloat16 [32, 32, 128], P('seq', 'groups'), parts along dimension 1, may hold values from -4 to 4
- values: bfloat16 [32, 32, 128], P('seq', 'groups'), parts along dimension 1, may hold values from -6 to 6
- cache_keys: bfloat16 [32, 2048, 128], P(('groups', 'seq')), parts along dimension 0, may hold values from -4 to 4
- cache_values: bfloat16 [32, 2048, 128], P(('groups', 'seq')), parts along dimension 0, may hold values from -6 to 6
- cache_len: int32 [32, 16], P(None, 'groups'), parts along dimension 1, may hold values from 1 to 2048, as said below
- out_weight: bfloat16 [2048, 2048], P('seq'), may hold values from -0.5 to 0.5
- norm_gain: bfloat16 [2048], replicated, may hold values from 0.5 to 1.5
- expert_ids: int32 [32, 16, 8], P('seq', 'groups'), parts along dimension 1, may hold values from 0 to 31, all different within a row; in each aligned block of 16 rows (0 to 15, 16 to 31, ..., all dimensions but the last counted through in order) at most 5 rows name the same one
- route_weights: float32 [32, 16, 8], P('seq', 'groups'), parts along dimension 1, may hold values from 0.02 to 1
- w_gate: bfloat16 [32, 2048, 384], P('seq'), may hold values from -0.125 to 0.125
- w_up: bfloat16 [32, 2048, 384], P('seq'), may hold values from -0.125 to 0.125
- w_down: bfloat16 [32, 384, 2048], P('seq'), may hold values from -0.3125 to 0.3125
Outputs:
- projected: bfloat16 [32, 16, 2048], P('seq', 'groups'), parts along dimension 1
- moe_out: bfloat16 [32, 16, 2048], P('seq', 'groups'), parts along dimension 1
There are 2 independent parts, one for each index of `groups`. A program takes and returns all parts, laid end to end along the dimension named above; an argument that names none is the same for every part. Nothing has to cross between parts.
Inputs may be any that keep to these rules, and one draw needn't show every extreme that they name: `cache_len`: every new token sees at least one cached key; some token sees all 2048. `expert_ids`: rows are taken position-major over members; in each aligned block of 16 rows (the rows of one index of seq) no expert is named more than 5 times, a bound that some block reaches.
All inputs are finite; a program needn't handle non-finite values.
Results may differ from a plain program's by a relative error of at most 0.01.
Values may be sent and summed in bfloat16 or wider, within the bound.
No kernel may reach another device: no remote copies, remote signals or barrier semaphores. Data moves between devices by JAX's collectives and lax.ppermute only.
A program may use at most 64 MiB of HBM per device.

v0:
```python
import jax
import jax.numpy as jnp
from jax import lax
from jax.sharding import PartitionSpec as P

D = 2048
HD = 128
TOPK = 8
QH = 16
KVH = 2
CAP = 5


def attend(query_heads, key_rows, value_rows, lengths):
    new_count = query_heads.shape[0]
    cache_count = key_rows.shape[0] - new_count
    scores = jnp.einsum(
        "qhd,kd->hqk", query_heads, key_rows, preferred_element_type=jnp.float32
    ) * HD ** (-0.5)
    cached_ok = jnp.arange(cache_count, dtype=jnp.int32)[None, :] < lengths[:, None]
    causal_ok = (
        jnp.arange(new_count, dtype=jnp.int32)[None, :]
        <= jnp.arange(new_count, dtype=jnp.int32)[:, None]
    )
    visible = jnp.concatenate([cached_ok, causal_ok], axis=1)
    scores = jnp.where(visible[None], scores, -1e30)
    row_max = jnp.max(scores, axis=-1, keepdims=True)
    expo = jnp.exp(scores - row_max)
    row_sum = jnp.sum(expo, axis=-1, keepdims=True)
    weights = (expo / row_sum).astype(jnp.bfloat16)
    result = jnp.einsum("hqk,kd->qhd", weights, value_rows, preferred_element_type=jnp.float32)
    return result.astype(jnp.bfloat16).reshape(new_count, -1)


def body(
    queries,
    keys,
    values,
    cache_keys,
    cache_values,
    cache_len,
    out_weight,
    norm_gain,
    expert_ids,
    route_weights,
    w_gate,
    w_up,
    w_down,
):
    slot_count = lax.axis_size("seq")
    per_rows = queries.shape[0]
    members = slot_count // KVH
    group_q = QH // KVH
    new_count = per_rows * slot_count
    position_index = lax.axis_index("seq")
    member = position_index // KVH
    query_rows, key_new, value_new = (
        lax.all_to_all(queries, "seq", split_axis=1, concat_axis=0, tiled=True),
        lax.all_to_all(keys, "seq", split_axis=1, concat_axis=0, tiled=True),
        lax.all_to_all(values, "seq", split_axis=1, concat_axis=0, tiled=True),
    )
    key_rows = jnp.concatenate([cache_keys[0], key_new.reshape(new_count, HD)], axis=0)
    value_rows = jnp.concatenate([cache_values[0], value_new.reshape(new_count, HD)], axis=0)
    lengths = lax.dynamic_slice_in_dim(cache_len, member, 1, 1)[:, 0]
    attended = attend(query_rows.reshape(new_count, group_q, HD), key_rows, value_rows, lengths)
    returned_heads = lax.all_to_all(
        attended[:, None, :], "seq", split_axis=0, concat_axis=1, tiled=True
    )
    token_heads = returned_heads.reshape(per_rows * members, QH * HD)
    projected_f = jnp.dot(
        token_heads,
        lax.all_gather(out_weight, "seq", axis=0, tiled=True),
        preferred_element_type=jnp.float32,
    )
    projected_f = projected_f.reshape(per_rows, members, D)
    projected = projected_f.astype(jnp.bfloat16)
    token_count = per_rows * members
    flat_rows = projected.reshape(token_count, D).astype(jnp.float32)
    stats = jnp.mean(flat_rows * flat_rows, axis=-1, keepdims=True)
    normed = (flat_rows * lax.rsqrt(stats + 1e-06) * norm_gain.astype(jnp.float32)).astype(
        jnp.bfloat16
    )
    exp_dev = w_gate.shape[0]
    expert_count = exp_dev * slot_count
    chosen_ids = expert_ids.reshape(token_count * TOPK)
    onehot = (chosen_ids[:, None] == jnp.arange(expert_count, dtype=jnp.int32)[None, :]).astype(
        jnp.int32
    )
    slot_rank = jnp.sum((jnp.cumsum(onehot, axis=0) - onehot) * onehot, axis=1)
    owner = chosen_ids // exp_dev
    local_expert = chosen_ids % exp_dev
    slot_target = (local_expert * slot_count + owner) * CAP + slot_rank
    total_slots = exp_dev * slot_count * CAP
    token_of = jnp.arange(token_count * TOPK, dtype=jnp.int32) // TOPK
    source_row = jnp.full((total_slots,), -1, jnp.int32).at[slot_target].set(token_of)
    filled = source_row >= 0
    outgoing = jnp.where(
        filled[:, None], normed[jnp.maximum(source_row, 0)], jnp.zeros((), jnp.bfloat16)
    )
    outgoing = outgoing.reshape(exp_dev, slot_count, CAP, D)
    incoming = lax.all_to_all(outgoing, "seq", split_axis=1, concat_axis=1, tiled=True)
    row_block = incoming.reshape(exp_dev, slot_count * CAP, D)
    gate_out = jnp.einsum("ecd,edf->ecf", row_block, w_gate, preferred_element_type=jnp.float32)
    up_out = jnp.einsum("ecd,edf->ecf", row_block, w_up, preferred_element_type=jnp.float32)
    hidden_act = (jax.nn.silu(gate_out) * up_out).astype(jnp.bfloat16)
    expert_out = jnp.einsum(
        "ecf,efd->ecd", hidden_act, w_down, preferred_element_type=jnp.float32
    ).astype(jnp.bfloat16)
    expert_back = lax.all_to_all(
        expert_out.reshape(exp_dev, slot_count, CAP, D),
        "seq",
        split_axis=1,
        concat_axis=1,
        tiled=True,
    )
    picked = expert_back.reshape(total_slots, D)[slot_target].reshape(token_count, TOPK, D)
    raw_weights = route_weights.reshape(token_count, TOPK)
    norm_weights = raw_weights / jnp.sum(raw_weights, axis=1, keepdims=True)
    mixed = jnp.sum(norm_weights[:, :, None] * picked.astype(jnp.float32), axis=1)
    moe_out = mixed.astype(jnp.bfloat16).reshape(per_rows, members, D)
    return (projected, moe_out)


def solution(mesh):
    return jax.shard_map(
        body,
        mesh=mesh,
        in_specs=(
            P("seq", "groups", None),
            P("seq", "groups", None),
            P("seq", "groups", None),
            P(("groups", "seq"), None, None),
            P(("groups", "seq"), None, None),
            P(None, "groups"),
            P("seq", None),
            P(),
            P("seq", "groups", None),
            P("seq", "groups", None),
            P("seq", None, None),
            P("seq", None, None),
            P("seq", None, None),
        ),
        out_specs=(P("seq", "groups", None), P("seq", "groups", None)),
        check_vma=False,
    )
```

profile of v0, /device:TPU:0, one launch (start us, length us, event | category | flops | bytes accessed | tf_op | source)
XLA Modules:
  0.0 167.0 jit_solution(5124968312826070863)
XLA Ops:
  7.2 0.0 copy-start
  7.2 0.0 all-gather.2.cloned.1.call-start
  7.2 0.7 all-gather.2.cloned.1.call-update
  7.9 1.7 %copy.33 = bf16[2,16,1024]{2,0,1:T(2,128)(2,1)} copy(bf16[2,16,1024]{2,1,0:T(8,128)(2,1)} %param.13) | data formatting | bytes 131072 | tf_op args[0]
  9.7 7.4 %all-to-all-start.2 = ((bf16[2,16,1024]{2,0,1:T(2,128)(2,1)}), bf16[2,16,1024]{2,0,1:T(2,128)(2,1)S(1)}, u32[]{:S(2)}, u32[]{:S(2)}) async-start(bf16[2,16,1024]{2,0,1:T(2,128)(2,1)} %copy.33), calls=%async_computation.2 | async-start | bytes 131072 | tf_op jit(solution)/shard_map/all_to_all | solution.py:58
  17.1 0.8 eq.17
  17.9 0.8 reshape.224
  18.7 0.1 fusion.31
  18.8 0.2 reduce_window_sum.11
  18.9 0.7 dynamic-slice_bitcast_fusion
  19.6 0.2 select_reduce_fusion
  19.8 0.1 iota_compare_fusion
  20.0 1.3 copy.32
  21.3 1.0 scatter_custom_fusion
  22.3 1.7 %all-to-all-done.2 = bf16[2,16,1024]{2,0,1:T(2,128)(2,1)S(1)} async-done(((bf16[2,16,1024]{2,0,1:T(2,128)(2,1)}), bf16[2,16,1024]{2,0,1:T(2,128)(2,1)S(1)}, u32[]{:S(2)}, u32[]{:S(2)}) %all-to-all-start.2) | async-done | bytes 65568 | tf_op jit(solution)/shard_map/all_to_all | solution.py:58
  24.0 4.3 %all-to-all-start.1 = ((bf16[2,16,128]{2,0,1:T(2,128)(2,1)}), bf16[2,16,128]{2,0,1:T(2,128)(2,1)S(1)}, u32[]{:S(2)}, u32[]{:S(2)}) async-start(bf16[2,16,128]{2,0,1:T(2,128)(2,1)} %copy.32), calls=%async_computation.1 | async-start | bytes 16384 | tf_op jit(solution)/shard_map/all_to_all | solution.py:59
  28.3 1.3 copy.31
  29.7 5.3 %all-to-all-done.1 = bf16[2,16,128]{2,0,1:T(2,128)(2,1)S(1)} async-done(((bf16[2,16,128]{2,0,1:T(2,128)(2,1)}), bf16[2,16,128]{2,0,1:T(2,128)(2,1)S(1)}, u32[]{:S(2)}, u32[]{:S(2)}) %all-to-all-start.1) | async-done | bytes 8224 | tf_op jit(solution)/shard_map/all_to_all | solution.py:59
  34.9 3.5 %all-to-all-start = ((bf16[2,16,128]{2,0,1:T(2,128)(2,1)}), bf16[2,16,128]{2,0,1:T(2,128)(2,1)S(1)}, u32[]{:S(2)}, u32[]{:S(2)}) async-start(bf16[2,16,128]{2,0,1:T(2,128)(2,1)} %copy.31), calls=%async_computation | async-start | bytes 16384 | tf_op jit(solution)/shard_map/all_to_all | solution.py:60
  38.4 3.4 %fusion.50 = (f32[8,32]{1,0:T(8,128)S(1)}, f32[8,32,2080]{2,1,0:T(8,128)}) fusion(pred[32,2080]{1,0:T(8,128)(4,1)S(1)} %pad_add_fusion, bf16[32,128]{1,0:T(8,128)(2,1)S(1)} %bitcast.89, bf16[2048,128]{1,0:T(8,128)(2,1)} %bitcast.91, bf16[32,8,128]{2,1,0:T(8,128)(2,1)S(1)} %reshape.222), kind=kOutput, calls=%fused_computation.81 | convolution fusion | flops 139511840 | bytes 2795520 | tf_op jit(solution)/shard_map/sub | solution.py:28
  41.8 2.9 %all-to-all-done = bf16[2,16,128]{2,0,1:T(2,128)(2,1)S(1)} async-done(((bf16[2,16,128]{2,0,1:T(2,128)(2,1)}), bf16[2,16,128]{2,0,1:T(2,128)(2,1)S(1)}, u32[]{:S(2)}, u32[]{:S(2)}) %all-to-all-start) | async-done | bytes 8224 | tf_op jit(solution)/shard_map/all_to_all | solution.py:60
  44.7 0.0 copy-start.5
  44.7 2.3 %fusion.11 = bf16[32,8,128]{2,0,1:T(8,128)(2,1)S(1)} fusion(f32[8,32,2080]{2,1,0:T(8,128)} %get-tuple-element.3, f32[8,32]{1,0:T(8,128)S(1)} %get-tuple-element.2, bf16[32,128]{1,0:T(8,128)(2,1)S(1)} %bitcast.90, bf16[2048,128]{1,0:T(8,128)(2,1)} %bitcast.92), kind=kOutput, calls=%fused_computation.17 | convolution fusion | flops 138477568 | bytes 2728960 | tf_op jit(solution)/shard_map/hqk,kd->qhd/dot_general | solution.py:31
  47.1 0.5 broadcast.188
  47.6 1.0 reduce.3
  48.6 0.7 reshape.261
  49.3 3.5 %all-to-all-start.3 = ((bf16[16,2,1024]{2,1,0:T(2,128)(2,1)}), bf16[16,2,1024]{2,1,0:T(2,128)(2,1)S(1)}, u32[]{:S(2)}, u32[]{:S(2)}) async-start(bf16[16,2,1024]{2,1,0:T(2,128)(2,1)} %reshape.261), calls=%async_computation.3 | async-start | bytes 131072 | tf_op jit(solution)/shard_map/all_to_all | solution.py:66
  52.8 0.0 copy-done.5
  52.8 0.1 broadcast_in_dim.49
  53.0 8.1 %all-to-all-done.3 = bf16[16,2,1024]{2,1,0:T(2,128)(2,1)S(1)} async-done(((bf16[16,2,1024]{2,1,0:T(2,128)(2,1)}), bf16[16,2,1024]{2,1,0:T(2,128)(2,1)S(1)}, u32[]{:S(2)}, u32[]{:S(2)}) %all-to-all-start.3) | async-done | bytes 65568 | tf_op jit(solution)/shard_map/all_to_all | solution.py:66
  61.1 0.1 reshape.262
  61.2 0.4 reduce.2
  61.6 26.4 %all-gather.2.cloned.1.call-done = bf16[2048,2048]{1,0:T(8,128)(2,1)} async-done(((bf16[128,2048]{1,0:T(8,128)(2,1)}), bf16[2048,2048]{1,0:T(8,128)(2,1)}) %all-gather.2.cloned.1.call-update) | async-done | bytes 8388624 | tf_op jit(solution)/shard_map/all_gather | solution.py:72
  88.0 4.7 %fusion.29 = (f32[2,8]{1,0:T(2,128)S(1)}, bf16[2,8,2048]{2,1,0:T(8,128)(2,1)S(1)}) fusion(bf16[2,8,2048]{2,1,0:T(8,128)(2,1)S(1)} %dot_general.22, bf16[2048,2048]{1,0:T(8,128)(2,1)} %all-gather.2.cloned.1.call-done), kind=kOutput, calls=%fused_computation.42 | convolution fusion | flops 134348784 | bytes 8519744 | tf_op jit(solution)/shard_map/dot_general | solution.py:70
  92.7 0.0 copy-start.3
  92.7 0.1 rsqrt.12
  92.8 0.1 fusion.28
  92.9 1.9 %gather_fusion = bf16[160,2048]{1,0:T(8,128)(2,1)} fusion(bf16[16,2048]{1,0:T(8,128)(2,1)S(1)} %fusion.28, s32[1024]{0:T(1024)S(1)} %pad_clamp_fusion.1), kind=kCustom, calls=%fused_computation | custom fusion | bytes 1311360 | tf_op jit(solution)/shard_map/gather | solution.py:98
  94.8 0.0 copy-done.3
  94.8 2.2 %gather.9 = bf16[2,16,5,2048]{3,2,1,0:T(8,128)(2,1)} reshape(bf16[160,2048]{1,0:T(8,128)(2,1)} %gather_fusion) | data formatting | bytes 1310720 | tf_op jit(solution)/shard_map/gather | solution.py:98
  97.0 0.0 copy-start.2
  97.0 1.5 broadcast_select_fusion
  98.6 0.7 copy.40
  99.3 21.4 %all_to_all.70 = bf16[2,16,5,2048]{3,0,2,1:T(2,128)(2,1)S(1)} all-to-all(bf16[2,16,5,2048]{3,0,2,1:T(2,128)(2,1)S(1)} %copy.40), channel_id=1, replica_groups=mesh['groups'=2,'seq'=16] {'seq'}, dimensions={1} | all-to-all | bytes 1310720 | tf_op jit(solution)/shard_map/all_to_all | solution.py:101
  120.7 0.0 copy-start.1
  120.7 0.9 copy-done.1
  121.5 0.0 copy-done.2
  121.5 0.8 fusion.15
  122.3 0.0 copy-done
  122.3 4.3 %convolution_convert_fusion = bf16[2,80,2048]{2,1,0:T(8,128)(2,1)} fusion(bf16[2,384,2048]{2,1,0:T(8,128)(2,1)S(1)} %copy-done, bf16[2,2048,384]{2,1,0:T(8,128)(2,1)} %param.24, bf16[2,80,2048]{2,0,1:T(2,128)(2,1)} %bitcast.83, f32[2,80,384]{2,1,0:T(8,128)S(1)} %fusion.15), kind=kOutput, calls=%fused_computation.11 | convolution fusion | flops 504012800 | bytes 7847936 | tf_op jit(solution)/shard_map/ecf,efd->ecd/dot_general | solution.py:106
  126.6 0.0 copy-start.4
  126.6 2.6 %copy.43 = bf16[2,80,2048]{2,0,1:T(2,128)(2,1)} copy(bf16[2,80,2048]{2,1,0:T(8,128)(2,1)} %convolution_convert_fusion) | data formatting | bytes 1310720 | tf_op jit(solution)/shard_map/convert_element_type | solution.py:108
  129.2 4.3 %all-to-all-start.5 = ((bf16[2,16,5,2048]{3,0,2,1:T(2,128)(2,1)}), bf16[2,16,5,2048]{3,0,2,1:T(2,128)(2,1)}, u32[]{:S(2)}, u32[]{:S(2)}) async-start(bf16[2,16,5,2048]{3,0,2,1:T(2,128)(2,1)} %bitcast.84), calls=%async_computation.5 | async-start | bytes 1310720 | tf_op jit(solution)/shard_map/all_to_all | solution.py:109
  133.5 0.0 copy-done.4
  133.5 0.1 copy.45
  133.6 0.1 reduce_sum.48
  133.7 0.1 div.58
  133.7 0.1 copy.39
  133.8 16.2 %all-to-all-done.5 = bf16[2,16,5,2048]{3,0,2,1:T(2,128)(2,1)} async-done(((bf16[2,16,5,2048]{3,0,2,1:T(2,128)(2,1)}), bf16[2,16,5,2048]{3,0,2,1:T(2,128)(2,1)}, u32[]{:S(2)}, u32[]{:S(2)}) %all-to-all-start.5) | async-done | bytes 655392 | tf_op jit(solution)/shard_map/all_to_all | solution.py:109
  150.1 2.4 %copy.44 = bf16[2,16,5,2048]{3,2,1,0:T(8,128)(2,1)} copy(bf16[2,16,5,2048]{3,0,2,1:T(2,128)(2,1)} %all-to-all-done.5) | data formatting | bytes 1310720 | tf_op jit(solution)/shard_map/all_to_all | solution.py:109
  152.4 2.2 %reshape.227 = bf16[160,2048]{1,0:T(8,128)(2,1)} reshape(bf16[2,16,5,2048]{3,2,1,0:T(8,128)(2,1)} %copy.44) | data formatting | bytes 1310720 | tf_op jit(solution)/shard_map/reshape | solution.py:116
  154.6 3.4 %gather_fusion.1 = bf16[128,2048]{1,0:T(8,128)(2,1)} fusion(bf16[160,2048]{1,0:T(8,128)(2,1)} %reshape.227, s32[1024]{0:T(1024)S(1)} %pad_clamp_fusion), kind=kCustom, calls=%fused_computation.1 | custom fusion | bytes 1049088 | tf_op jit(solution)/shard_map/gather | solution.py:116
  158.0 2.1 %fusion.12 = bf16[16,2048]{1,0:T(8,128)(2,1)} fusion(bf16[128,2048]{1,0:T(8,128)(2,1)} %gather_fusion.1, f32[16,8]{1,0:T(8,128)S(1)} %copy.39), kind=kLoop, calls=%fused_computation.19 | loop fusion | flops 753664 | bytes 590336 | tf_op jit(solution)/shard_map/reduce_sum | solution.py:119
  (17 shorter events, 0.3 us)
Async XLA Ops:
  7.2 115.2 %copy-start = (bf16[2,384,2048]{2,1,0:T(8,128)(2,1)S(1)}, bf16[2,384,2048]{2,1,0:T(8,128)(2,1)}, u32[]{:S(2)}) copy-start(bf16[2,384,2048]{2,1,0:T(8,128)(2,1)} %param.25) | copy-start | bytes 9437188
  7.2 80.9 %all-gather.2.cloned.1.call-start = ((), (), s32[]{:S(2)}) async-start(), calls=%async_computation.6 | async-start | bytes 8912896 | tf_op jit(solution)/shard_map/all_gather | solution.py:72
  9.7 14.3 %all-to-all-start.2 = ((bf16[2,16,1024]{2,0,1:T(2,128)(2,1)}), bf16[2,16,1024]{2,0,1:T(2,128)(2,1)S(1)}, u32[]{:S(2)}, u32[]{:S(2)}) async-start(bf16[2,16,1024]{2,0,1:T(2,128)(2,1)} %copy.33), calls=%async_computation.2 | async-start | bytes 131072 | tf_op jit(solution)/shard_map/all_to_all | solution.py:58
  24.0 10.9 %all-to-all-start.1 = ((bf16[2,16,128]{2,0,1:T(2,128)(2,1)}), bf16[2,16,128]{2,0,1:T(2,128)(2,1)S(1)}, u32[]{:S(2)}, u32[]{:S(2)}) async-start(bf16[2,16,128]{2,0,1:T(2,128)(2,1)} %copy.32), calls=%async_computation.1 | async-start | bytes 16384 | tf_op jit(solution)/shard_map/all_to_all | solution.py:59
  34.9 9.8 %all-to-all-start = ((bf16[2,16,128]{2,0,1:T(2,128)(2,1)}), bf16[2,16,128]{2,0,1:T(2,128)(2,1)S(1)}, u32[]{:S(2)}, u32[]{:S(2)}) async-start(bf16[2,16,128]{2,0,1:T(2,128)(2,1)} %copy.31), calls=%async_computation | async-start | bytes 16384 | tf_op jit(solution)/shard_map/all_to_all | solution.py:60
  44.7 8.1 %copy-start.5 = (bf16[2048]{0:T(1024)(128)(2,1)S(1)}, bf16[2048]{0:T(1024)(128)(2,1)}, u32[]{:S(2)}) copy-start(bf16[2048]{0:T(1024)(128)(2,1)} %param.20) | copy-start | bytes 12292
  49.3 11.8 %all-to-all-start.3 = ((bf16[16,2,1024]{2,1,0:T(2,128)(2,1)}), bf16[16,2,1024]{2,1,0:T(2,128)(2,1)S(1)}, u32[]{:S(2)}, u32[]{:S(2)}) async-start(bf16[16,2,1024]{2,1,0:T(2,128)(2,1)} %reshape.261), calls=%async_computation.3 | async-start | bytes 131072 | tf_op jit(solution)/shard_map/all_to_all | solution.py:66
  92.7 2.1 %copy-start.3 = (bf16[2,8,2048]{2,1,0:T(8,128)(2,1)}, bf16[2,8,2048]{2,1,0:T(8,128)(2,1)S(1)}, u32[]{:S(2)}) copy-start(bf16[2,8,2048]{2,1,0:T(8,128)(2,1)S(1)} %get-tuple-element.5) | copy-start | bytes 196612
  97.0 24.5 %copy-start.2 = (bf16[2,2048,384]{2,1,0:T(8,128)(2,1)S(1)}, bf16[2,2048,384]{2,1,0:T(8,128)(2,1)}, u32[]{:S(2)}) copy-start(bf16[2,2048,384]{2,1,0:T(8,128)(2,1)} %param.23) | copy-start | bytes 9437188
  120.7 0.9 copy-start.1
  126.6 6.9 %copy-start.4 = (f32[2,8,8]{2,1,0:T(8,128)S(1)}, f32[2,8,8]{2,1,0:T(8,128)}, u32[]{:S(2)}) copy-start(f32[2,8,8]{2,1,0:T(8,128)} %param.22) | copy-start | bytes 1540
  129.2 20.9 %all-to-all-start.5 = ((bf16[2,16,5,2048]{3,0,2,1:T(2,128)(2,1)}), bf16[2,16,5,2048]{3,0,2,1:T(2,128)(2,1)}, u32[]{:S(2)}, u32[]{:S(2)}) async-start(bf16[2,16,5,2048]{3,0,2,1:T(2,128)(2,1)} %bitcast.84), calls=%async_computation.5 | async-start | bytes 1310720 | tf_op jit(solution)/shard_map/all_to_all | solution.py:109
Sparse Core Ops, SparseCore 0:
  10.2 77.8 all-gather.1
where the time goes:
time: 168 us; the launch traced here: 167 us
  waiting for transfers between devices  61.4 us (37%)
  local copies, waits for them, and re-layouts  25.7 us (15%)
  starting transfers between devices  23 us (14%)
  blocking collectives  21.4 us (13%)
  matrix products  15.4 us (9%)
  between operations  14.3 us (9%)
  other arithmetic  5.82 us (3%)
    all_gather x1, waiting for transfers between devices, body(): lax.all_gather(out_weight, 'seq', axis=0, tiled=True)  26.4 us
    all_to_all x1, blocking collectives, body(): lax.all_to_all(outgoing, 'seq', split_axis=1, concat_axis=1, tiled=True)  21.4 us
    all_to_all x1, waiting for transfers between devices, body(): lax.all_to_all(expert_out.reshape(exp_dev, slot_count, CAP, D), 'seq', sp...  16.2 us
    all_to_all x1, waiting for transfers between devices, body(): lax.all_to_all(attended[:, None, :], 'seq', split_axis=0, concat_axis=1,...  8.13 us
    all_to_all x1, starting transfers between devices, body(): lax.all_to_all(queries, 'seq', split_axis=1, concat_axis=0, tiled=True)  7.41 us
    unnamed x17, local copies, waits for them, and re-layouts  5.94 us
    all_to_all x1, waiting for transfers between devices, body(): lax.all_to_all(keys, 'seq', split_axis=1, concat_axis=0, tiled=True)  5.26 us
    dot_general x1, matrix products, body(): jnp.dot(token_heads, lax.all_gather(out_weight, 'seq', axis=0, tiled=True...  4.66 us
  transfers between devices with their start and end apart: 6, of which 6 were waited for; matrix products, arithmetic and copies ran while one was open for 10% of the time, Pallas kernels for 0%

commit v1 on v0

--- a/solution.py
+++ b/solution.py
@@ -9,6 +9,17 @@
 QH = 16
 KVH = 2
 CAP = 5
+
+
+def cut_along(shard, dim, size):
+    before, after = (shard.shape[:dim], shard.shape[dim + 1 :])
+    return jnp.moveaxis(shard.reshape(*before, size, -1, *after), dim, 0)
+
+
+def joined_along(blocks, dim):
+    blocks = jnp.moveaxis(blocks, 0, dim)
+    lengths = blocks.shape
+    return blocks.reshape(*lengths[:dim], lengths[dim] * lengths[dim + 1], *lengths[dim + 2 :])
 
 
 def attend(query_heads, key_rows, value_rows, lengths):
@@ -63,9 +74,15 @@
     value_rows = jnp.concatenate([cache_values[0], value_new.reshape(new_count, HD)], axis=0)
     lengths = lax.dynamic_slice_in_dim(cache_len, member, 1, 1)[:, 0]
     attended = attend(query_rows.reshape(new_count, group_q, HD), key_rows, value_rows, lengths)
-    returned_heads = lax.all_to_all(
-        attended[:, None, :], "seq", split_axis=0, concat_axis=1, tiled=True
-    )
+    array = attended[:, None, :]
+    peers, mine = (lax.axis_size("seq"), lax.axis_index("seq"))
+    tiles = cut_along(array, 0, peers)
+    outs = [tiles[mine]]
+    for step in range(1, peers):
+        sent = tiles[mine ^ step]
+        outs.append(lax.ppermute(sent, "seq", [(i, i ^ step) for i in range(peers)]))
+    tiles = jnp.stack(outs)[mine ^ jnp.arange(peers)]
+    returned_heads = joined_along(tiles, 1)
     token_heads = returned_heads.reshape(per_rows * members, QH * HD)
     projected_f = jnp.dot(
         token_heads,

time: 168 us -> 168 us (level)
  starting transfers between devices: 23 us -> 40.6 us
  waiting for transfers between devices: 61.4 us -> 45.4 us
    ppermute x0 -> x15, starting transfers between devices: none -> 21.1 us  [body(): lax.ppermute(sent, 'seq', [(i, i ^ step) for i in range(peers)])]
    all_gather x1, waiting for transfers between devices: 26.4 us -> 15.6 us  [body(): lax.all_gather(out_weight, 'seq', axis=0, tiled=True)]
    all_to_all x1 -> x0, waiting for transfers between devices: 8.13 us -> none  [body(): lax.all_to_all(attended[:, None, :], 'seq', split_axis=0, concat_axis=1,...]
    all_to_all x1 -> x0, starting transfers between devices: 3.5 us -> none  [body(): lax.all_to_all(attended[:, None, :], 'seq', split_axis=0, concat_axis=1,...]
    ppermute x0 -> x15, waiting for transfers between devices: none -> 3.15 us  [body(): lax.ppermute(sent, 'seq', [(i, i ^ step) for i in range(peers)])]
    unnamed x17 -> x29, local copies, waits for them, and re-layouts: 5.94 us -> 5.4 us
  transfers between devices with their start and end apart: 6 -> 20, of which waited for: 6 -> 7; matrix products, arithmetic and copies ran while one was open for 10% -> 9% of each run, Pallas kernels for 0% -> 0%
where the time goes in v1:
time: 168 us; the launch traced here: 167 us
  waiting for transfers between devices  45.4 us (27%)
  starting transfers between devices  40.6 us (24%)
  local copies, waits for them, and re-layouts  25.5 us (15%)
  blocking collectives  21.3 us (13%)
  matrix products  15.4 us (9%)
  between operations  14.4 us (9%)
  other arithmetic  4.46 us (3%)
    all_to_all x1, blocking collectives, body(): lax.all_to_all(outgoing, 'seq', split_axis=1, concat_axis=1, tiled=True)  21.3 us
    ppermute x15, starting transfers between devices, body(): lax.ppermute(sent, 'seq', [(i, i ^ step) for i in range(peers)])  21.1 us
    all_to_all x1, waiting for transfers between devices, body(): lax.all_to_all(expert_out.reshape(exp_dev, slot_count, CAP, D), 'seq', sp...  16.2 us
    all_gather x1, waiting for transfers between devices, body(): lax.all_gather(out_weight, 'seq', axis=0, tiled=True)  15.6 us
    all_to_all x1, starting transfers between devices, body(): lax.all_to_all(queries, 'seq', split_axis=1, concat_axis=0, tiled=True)  7.41 us
    unnamed x29, local copies, waits for them, and re-layouts  5.4 us
    all_to_all x1, waiting for transfers between devices, body(): lax.all_to_all(keys, 'seq', split_axis=1, concat_axis=0, tiled=True)  5.19 us
    dot_general x1, matrix products, body(): jnp.dot(token_heads, lax.all_gather(out_weight, 'seq', axis=0, tiled=True...  4.66 us
  transfers between devices with their start and end apart: 20, of which 7 were waited for; matrix products, arithmetic and copies ran while one was open for 9% of the time, Pallas kernels for 0%

profile of v1, /device:TPU:0, one launch (start us, length us, event | category | flops | bytes accessed | tf_op | source)
XLA Modules:
  0.0 167.2 jit_solution(11830878689470445380)
XLA Ops:
  7.2 0.0 all-gather.2.cloned.1.call-start
  7.2 0.7 all-gather.2.cloned.1.call-update
  7.9 1.7 %copy.79 = bf16[2,16,1024]{2,0,1:T(2,128)(2,1)} copy(bf16[2,16,1024]{2,1,0:T(8,128)(2,1)} %param.13) | data formatting | bytes 131072 | tf_op args[0]
  9.7 7.4 %all-to-all-start.2 = ((bf16[2,16,1024]{2,0,1:T(2,128)(2,1)}), bf16[2,16,1024]{2,0,1:T(2,128)(2,1)S(1)}, u32[]{:S(2)}, u32[]{:S(2)}) async-start(bf16[2,16,1024]{2,0,1:T(2,128)(2,1)} %copy.79), calls=%async_computation.2 | async-start | bytes 131072 | tf_op jit(solution)/shard_map/all_to_all | solution.py:69
  17.1 0.8 eq.17
  17.9 0.8 reshape.238
  18.7 0.1 fusion.31
  18.8 0.2 reduce_window_sum.11
  18.9 0.2 select_reduce_fusion
  19.1 1.0 scatter_custom_fusion
  20.1 0.7 fusion.57
  20.8 0.1 iota_compare_fusion
  21.0 1.3 copy.78
  22.3 1.7 %all-to-all-done.2 = bf16[2,16,1024]{2,0,1:T(2,128)(2,1)S(1)} async-done(((bf16[2,16,1024]{2,0,1:T(2,128)(2,1)}), bf16[2,16,1024]{2,0,1:T(2,128)(2,1)S(1)}, u32[]{:S(2)}, u32[]{:S(2)}) %all-to-all-start.2) | async-done | bytes 65568 | tf_op jit(solution)/shard_map/all_to_all | solution.py:69
  24.0 4.3 %all-to-all-start.1 = ((bf16[2,16,128]{2,0,1:T(2,128)(2,1)}), bf16[2,16,128]{2,0,1:T(2,128)(2,1)S(1)}, u32[]{:S(2)}, u32[]{:S(2)}) async-start(bf16[2,16,128]{2,0,1:T(2,128)(2,1)} %copy.78), calls=%async_computation.1 | async-start | bytes 16384 | tf_op jit(solution)/shard_map/all_to_all | solution.py:70
  28.4 1.3 copy.77
  29.8 5.2 %all-to-all-done.1 = bf16[2,16,128]{2,0,1:T(2,128)(2,1)S(1)} async-done(((bf16[2,16,128]{2,0,1:T(2,128)(2,1)}), bf16[2,16,128]{2,0,1:T(2,128)(2,1)S(1)}, u32[]{:S(2)}, u32[]{:S(2)}) %all-to-all-start.1) | async-done | bytes 8224 | tf_op jit(solution)/shard_map/all_to_all | solution.py:70
  34.9 3.5 %all-to-all-start = ((bf16[2,16,128]{2,0,1:T(2,128)(2,1)}), bf16[2,16,128]{2,0,1:T(2,128)(2,1)S(1)}, u32[]{:S(2)}, u32[]{:S(2)}) async-start(bf16[2,16,128]{2,0,1:T(2,128)(2,1)} %copy.77), calls=%async_computation | async-start | bytes 16384 | tf_op jit(solution)/shard_map/all_to_all | solution.py:71
  38.4 3.4 %fusion.67 = (f32[8,32]{1,0:T(8,128)S(1)}, f32[8,32,2080]{2,1,0:T(8,128)}) fusion(pred[32,2080]{1,0:T(8,128)(4,1)S(1)} %pad_add_fusion, bf16[32,128]{1,0:T(8,128)(2,1)S(1)} %bitcast.185, bf16[2048,128]{1,0:T(8,128)(2,1)} %bitcast.187, bf16[32,8,128]{2,1,0:T(8,128)(2,1)S(1)} %reshape.236), kind=kOutput, calls=%fused_computation.133 | convolution fusion | flops 139511840 | bytes 2795520 | tf_op jit(solution)/shard_map/sub | solution.py:39
  41.8 2.9 %all-to-all-done = bf16[2,16,128]{2,0,1:T(2,128)(2,1)S(1)} async-done(((bf16[2,16,128]{2,0,1:T(2,128)(2,1)}), bf16[2,16,128]{2,0,1:T(2,128)(2,1)S(1)}, u32[]{:S(2)}, u32[]{:S(2)}) %all-to-all-start) | async-done | bytes 8224 | tf_op jit(solution)/shard_map/all_to_all | solution.py:71
  44.7 2.3 %fusion.11 = bf16[32,8,128]{2,0,1:T(8,128)(2,1)S(1)} fusion(f32[8,32,2080]{2,1,0:T(8,128)} %get-tuple-element.19, f32[8,32]{1,0:T(8,128)S(1)} %get-tuple-element.18, bf16[32,128]{1,0:T(8,128)(2,1)S(1)} %bitcast.186, bf16[2048,128]{1,0:T(8,128)(2,1)} %bitcast.188), kind=kOutput, calls=%fused_computation.18 | convolution fusion | flops 138477568 | bytes 2728960 | tf_op jit(solution)/shard_map/hqk,kd->qhd/dot_general | solution.py:42
  47.1 0.1 fusion.52
  47.3 0.1 collective-permute-start
  47.4 0.1 broadcast_in_dim.50
  47.5 0.6 collective-permute-start.1
  48.0 1.3 collective-permute-start.2
  49.4 0.5 collective-permute-start.3
  49.9 1.1 collective-permute-start.4
  51.0 0.5 collective-permute-start.5
  51.6 2.3 %collective-permute-start.6 = (bf16[2,1,1024]{2,0,1:T(2,128)(2,1)S(1)}, bf16[2,1,1024]{2,0,1:T(2,128)(2,1)S(1)}, u32[]{:S(2)}, u32[]{:S(2)}) collective-permute-start(bf16[2,1,1024]{2,0,1:T(2,128)(2,1)S(1)} %get-tuple-element.10), channel_id=1, source_target_pairs={{0,7},{1,6},{2,5},{3,4},{4,3},{5,2},{6,1},{7,0},{8,15},{9,14},{10,... | collective-permute-start | bytes 12296 | tf_op jit(solution)/shard_map/ppermute | solution.py:83
  53.9 0.6 collective-permute-start.7
  54.5 2.1 %collective-permute-start.8 = (bf16[2,1,1024]{2,0,1:T(2,128)(2,1)S(1)}, bf16[2,1,1024]{2,0,1:T(2,128)(2,1)S(1)}, u32[]{:S(2)}, u32[]{:S(2)}) collective-permute-start(bf16[2,1,1024]{2,0,1:T(2,128)(2,1)S(1)} %get-tuple-element.8), channel_id=1, source_target_pairs={{0,9},{1,8},{2,11},{3,10},{4,13},{5,12},{6,15},{7,14},{8,1},{9,0},... | collective-permute-start | bytes 12296 | tf_op jit(solution)/shard_map/ppermute | solution.py:83
  56.6 0.9 collective-permute-start.9
  57.5 2.8 %collective-permute-start.10 = (bf16[2,1,1024]{2,0,1:T(2,128)(2,1)S(1)}, bf16[2,1,1024]{2,0,1:T(2,128)(2,1)S(1)}, u32[]{:S(2)}, u32[]{:S(2)}) collective-permute-start(bf16[2,1,1024]{2,0,1:T(2,128)(2,1)S(1)} %get-tuple-element.6), channel_id=1, source_target_pairs={{0,11},{1,10},{2,9},{3,8},{4,15},{5,14},{6,13},{7,12},{8,3},{9,2},... | collective-permute-start | bytes 12296 | tf_op jit(solution)/shard_map/ppermute | solution.py:83
  60.4 0.8 collective-permute-start.11
  61.2 2.7 %collective-permute-start.12 = (bf16[2,1,1024]{2,0,1:T(2,128)(2,1)S(1)}, bf16[2,1,1024]{2,0,1:T(2,128)(2,1)S(1)}, u32[]{:S(2)}, u32[]{:S(2)}) collective-permute-start(bf16[2,1,1024]{2,0,1:T(2,128)(2,1)S(1)} %get-tuple-element.4), channel_id=1, source_target_pairs={{0,13},{1,12},{2,15},{3,14},{4,9},{5,8},{6,11},{7,10},{8,5},{9,4},... | collective-permute-start | bytes 12296 | tf_op jit(solution)/shard_map/ppermute | solution.py:83
  64.0 1.9 %collective-permute-start.13 = (bf16[2,1,1024]{2,0,1:T(2,128)(2,1)S(1)}, bf16[2,1,1024]{2,0,1:T(2,128)(2,1)S(1)}, u32[]{:S(2)}, u32[]{:S(2)}) collective-permute-start(bf16[2,1,1024]{2,0,1:T(2,128)(2,1)S(1)} %get-tuple-element.3), channel_id=1, source_target_pairs={{0,14},{1,15},{2,12},{3,13},{4,10},{5,11},{6,8},{7,9},{8,6},{9,7},... | collective-permute-start | bytes 12296 | tf_op jit(solution)/shard_map/ppermute | solution.py:83
  65.9 2.8 %collective-permute-start.14 = (bf16[2,1,1024]{2,0,1:T(2,128)(2,1)S(1)}, bf16[2,1,1024]{2,0,1:T(2,128)(2,1)S(1)}, u32[]{:S(2)}, u32[]{:S(2)}) collective-permute-start(bf16[2,1,1024]{2,0,1:T(2,128)(2,1)S(1)} %get-tuple-element.2), channel_id=1, source_target_pairs={{0,15},{1,14},{2,13},{3,12},{4,11},{5,10},{6,9},{7,8},{8,7},{9,6},... | collective-permute-start | bytes 12296 | tf_op jit(solution)/shard_map/ppermute | solution.py:83
  68.7 1.8 %collective-permute-done.13 = bf16[2,1,1024]{2,0,1:T(2,128)(2,1)S(1)} collective-permute-done((bf16[2,1,1024]{2,0,1:T(2,128)(2,1)S(1)}, bf16[2,1,1024]{2,0,1:T(2,128)(2,1)S(1)}, u32[]{:S(2)}, u32[]{:S(2)}) %collective-permute-start.13) | collective-permute-done | bytes 4128 | tf_op jit(solution)/shard_map/ppermute | solution.py:83
  70.6 1.3 collective-permute-done.14
  71.9 0.7 gather_fusion
  72.6 15.6 %all-gather.2.cloned.1.call-done = bf16[2048,2048]{1,0:T(8,128)(2,1)} async-done(((bf16[128,2048]{1,0:T(8,128)(2,1)}), bf16[2048,2048]{1,0:T(8,128)(2,1)}) %all-gather.2.cloned.1.call-update) | async-done | bytes 8388624 | tf_op jit(solution)/shard_map/all_gather | solution.py:89
  88.2 4.7 %fusion.29 = (f32[2,8]{1,0:T(2,128)S(1)}, bf16[2,8,2048]{2,1,0:T(8,128)(2,1)S(1)}) fusion(bf16[2,8,2048]{2,1,0:T(8,128)(2,1)S(1)} %dot_general.22, bf16[2048,2048]{1,0:T(8,128)(2,1)} %all-gather.2.cloned.1.call-done), kind=kOutput, calls=%fused_computation.43 | convolution fusion | flops 134348784 | bytes 8519744 | tf_op jit(solution)/shard_map/dot_general | solution.py:87
  92.9 0.1 rsqrt.12
  93.0 0.1 fusion.28
  93.1 1.9 %gather_fusion.1 = bf16[160,2048]{1,0:T(8,128)(2,1)} fusion(bf16[16,2048]{1,0:T(8,128)(2,1)S(1)} %fusion.28, s32[1024]{0:T(1024)S(1)} %pad_clamp_fusion.1), kind=kCustom, calls=%fused_computation.1 | custom fusion | bytes 1311360 | tf_op jit(solution)/shard_map/gather | solution.py:115
  95.0 2.2 %gather.13 = bf16[2,16,5,2048]{3,2,1,0:T(8,128)(2,1)} reshape(bf16[160,2048]{1,0:T(8,128)(2,1)} %gather_fusion.1) | data formatting | bytes 1310720 | tf_op jit(solution)/shard_map/gather | solution.py:115
  97.2 1.5 broadcast_select_fusion
  98.8 0.7 copy.102
  99.5 21.3 %all_to_all.55 = bf16[2,16,5,2048]{3,0,2,1:T(2,128)(2,1)S(1)} all-to-all(bf16[2,16,5,2048]{3,0,2,1:T(2,128)(2,1)S(1)} %copy.102), channel_id=1, replica_groups=mesh['groups'=2,'seq'=16] {'seq'}, dimensions={1} | all-to-all | bytes 1310720 | tf_op jit(solution)/shard_map/all_to_all | solution.py:118
  120.8 0.9 copy-done.1
  121.7 0.8 fusion.15
  122.5 4.3 %convolution_convert_fusion = bf16[2,80,2048]{2,1,0:T(8,128)(2,1)} fusion(bf16[2,384,2048]{2,1,0:T(8,128)(2,1)S(1)} %copy-done, bf16[2,2048,384]{2,1,0:T(8,128)(2,1)} %param.24, bf16[2,80,2048]{2,0,1:T(2,128)(2,1)} %bitcast.178, f32[2,80,384]{2,1,0:T(8,128)S(1)} %fusion.15), kind=kOutput, calls=%fused_computation.12 | convolution fusion | flops 504012800 | bytes 7847936 | tf_op jit(solution)/shard_map/ecf,efd->ecd/dot_general | solution.py:123
  126.8 2.6 %copy.105 = bf16[2,80,2048]{2,0,1:T(2,128)(2,1)} copy(bf16[2,80,2048]{2,1,0:T(8,128)(2,1)} %convolution_convert_fusion) | data formatting | bytes 1310720 | tf_op jit(solution)/shard_map/convert_element_type | solution.py:125
  129.4 4.3 %all-to-all-start.4 = ((bf16[2,16,5,2048]{3,0,2,1:T(2,128)(2,1)}), bf16[2,16,5,2048]{3,0,2,1:T(2,128)(2,1)}, u32[]{:S(2)}, u32[]{:S(2)}) async-start(bf16[2,16,5,2048]{3,0,2,1:T(2,128)(2,1)} %bitcast.179), calls=%async_computation.4 | async-start | bytes 1310720 | tf_op jit(solution)/shard_map/all_to_all | solution.py:126
  133.6 0.1 copy.108
  133.7 0.1 reduce_sum.48
  133.8 0.1 div.58
  133.9 0.1 copy.101
  134.0 16.2 %all-to-all-done.4 = bf16[2,16,5,2048]{3,0,2,1:T(2,128)(2,1)} async-done(((bf16[2,16,5,2048]{3,0,2,1:T(2,128)(2,1)}), bf16[2,16,5,2048]{3,0,2,1:T(2,128)(2,1)}, u32[]{:S(2)}, u32[]{:S(2)}) %all-to-all-start.4) | async-done | bytes 655392 | tf_op jit(solution)/shard_map/all_to_all | solution.py:126
  150.2 2.4 %copy.106 = bf16[2,16,5,2048]{3,2,1,0:T(8,128)(2,1)} copy(bf16[2,16,5,2048]{3,0,2,1:T(2,128)(2,1)} %all-to-all-done.4) | data formatting | bytes 1310720 | tf_op jit(solution)/shard_map/all_to_all | solution.py:126
  152.6 2.2 %reshape.241 = bf16[160,2048]{1,0:T(8,128)(2,1)} reshape(bf16[2,16,5,2048]{3,2,1,0:T(8,128)(2,1)} %copy.106) | data formatting | bytes 1310720 | tf_op jit(solution)/shard_map/reshape | solution.py:133
  154.8 3.4 %gather_fusion.2 = bf16[128,2048]{1,0:T(8,128)(2,1)} fusion(bf16[160,2048]{1,0:T(8,128)(2,1)} %reshape.241, s32[1024]{0:T(1024)S(1)} %pad_clamp_fusion), kind=kCustom, calls=%fused_computation.2 | custom fusion | bytes 1049088 | tf_op jit(solution)/shard_map/gather | solution.py:133
  158.2 2.1 %fusion.12 = bf16[16,2048]{1,0:T(8,128)(2,1)} fusion(bf16[128,2048]{1,0:T(8,128)(2,1)} %gather_fusion.2, f32[16,8]{1,0:T(8,128)S(1)} %copy.101), kind=kLoop, calls=%fused_computation.20 | loop fusion | flops 753664 | bytes 590336 | tf_op jit(solution)/shard_map/reduce_sum | solution.py:136
  (57 shorter events, 0.5 us)
Async XLA Ops:
  7.2 115.3 %copy-start = (bf16[2,384,2048]{2,1,0:T(8,128)(2,1)S(1)}, bf16[2,384,2048]{2,1,0:T(8,128)(2,1)}, u32[]{:S(2)}) copy-start(bf16[2,384,2048]{2,1,0:T(8,128)(2,1)} %param.25) | copy-start | bytes 9437188
  7.2 81.1 %all-gather.2.cloned.1.call-start = ((), (), s32[]{:S(2)}) async-start(), calls=%async_computation.5 | async-start | bytes 8912896 | tf_op jit(solution)/shard_map/all_gather | solution.py:89
  9.7 14.3 %all-to-all-start.2 = ((bf16[2,16,1024]{2,0,1:T(2,128)(2,1)}), bf16[2,16,1024]{2,0,1:T(2,128)(2,1)S(1)}, u32[]{:S(2)}, u32[]{:S(2)}) async-start(bf16[2,16,1024]{2,0,1:T(2,128)(2,1)} %copy.79), calls=%async_computation.2 | async-start | bytes 131072 | tf_op jit(solution)/shard_map/all_to_all | solution.py:69
  24.0 11.0 %all-to-all-start.1 = ((bf16[2,16,128]{2,0,1:T(2,128)(2,1)}), bf16[2,16,128]{2,0,1:T(2,128)(2,1)S(1)}, u32[]{:S(2)}, u32[]{:S(2)}) async-start(bf16[2,16,128]{2,0,1:T(2,128)(2,1)} %copy.78), calls=%async_computation.1 | async-start | bytes 16384 | tf_op jit(solution)/shard_map/all_to_all | solution.py:70
  34.9 9.8 %all-to-all-start = ((bf16[2,16,128]{2,0,1:T(2,128)(2,1)}), bf16[2,16,128]{2,0,1:T(2,128)(2,1)S(1)}, u32[]{:S(2)}, u32[]{:S(2)}) async-start(bf16[2,16,128]{2,0,1:T(2,128)(2,1)} %copy.77), calls=%async_computation | async-start | bytes 16384 | tf_op jit(solution)/shard_map/all_to_all | solution.py:71
  44.7 2.6 %copy-start.5 = (bf16[2048]{0:T(1024)(128)(2,1)S(1)}, bf16[2048]{0:T(1024)(128)(2,1)}, u32[]{:S(2)}) copy-start(bf16[2048]{0:T(1024)(128)(2,1)} %param.20) | copy-start | bytes 12292
  47.3 3.8 %collective-permute-start = (bf16[2,1,1024]{2,0,1:T(2,128)(2,1)S(1)}, bf16[2,1,1024]{2,0,1:T(2,128)(2,1)S(1)}, u32[]{:S(2)}, u32[]{:S(2)}) collective-permute-start(bf16[2,1,1024]{2,0,1:T(2,128)(2,1)S(1)} %get-tuple-element.16), channel_id=1, source_target_pairs={{0,1},{1,0},{2,3},{3,2},{4,5},{5,4},{6,7},{7,6},{8,9},{9,8},{10,11... | collective-permute-start | bytes 12296 | tf_op jit(solution)/shard_map/ppermute | solution.py:83
  47.5 4.1 %collective-permute-start.1 = (bf16[2,1,1024]{2,0,1:T(2,128)(2,1)S(1)}, bf16[2,1,1024]{2,0,1:T(2,128)(2,1)S(1)}, u32[]{:S(2)}, u32[]{:S(2)}) collective-permute-start(bf16[2,1,1024]{2,0,1:T(2,128)(2,1)S(1)} %get-tuple-element.15), channel_id=1, source_target_pairs={{0,2},{1,3},{2,0},{3,1},{4,6},{5,7},{6,4},{7,5},{8,10},{9,11},{10,... | collective-permute-start | bytes 12296 | tf_op jit(solution)/shard_map/ppermute | solution.py:83
  48.0 5.8 %collective-permute-start.2 = (bf16[2,1,1024]{2,0,1:T(2,128)(2,1)S(1)}, bf16[2,1,1024]{2,0,1:T(2,128)(2,1)S(1)}, u32[]{:S(2)}, u32[]{:S(2)}) collective-permute-start(bf16[2,1,1024]{2,0,1:T(2,128)(2,1)S(1)} %get-tuple-element.14), channel_id=1, source_target_pairs={{0,3},{1,2},{2,1},{3,0},{4,7},{5,6},{6,5},{7,4},{8,11},{9,10},{10,... | collective-permute-start | bytes 12296 | tf_op jit(solution)/shard_map/ppermute | solution.py:83
  49.4 5.1 %collective-permute-start.3 = (bf16[2,1,1024]{2,0,1:T(2,128)(2,1)S(1)}, bf16[2,1,1024]{2,0,1:T(2,128)(2,1)S(1)}, u32[]{:S(2)}, u32[]{:S(2)}) collective-permute-start(bf16[2,1,1024]{2,0,1:T(2,128)(2,1)S(1)} %get-tuple-element.13), channel_id=1, source_target_pairs={{0,4},{1,5},{2,6},{3,7},{4,0},{5,1},{6,2},{7,3},{8,12},{9,13},{10,... | collective-permute-start | bytes 12296 | tf_op jit(solution)/shard_map/ppermute | solution.py:83
  49.9 6.7 %collective-permute-start.4 = (bf16[2,1,1024]{2,0,1:T(2,128)(2,1)S(1)}, bf16[2,1,1024]{2,0,1:T(2,128)(2,1)S(1)}, u32[]{:S(2)}, u32[]{:S(2)}) collective-permute-start(bf16[2,1,1024]{2,0,1:T(2,128)(2,1)S(1)} %get-tuple-element.12), channel_id=1, source_target_pairs={{0,5},{1,4},{2,7},{3,6},{4,1},{5,0},{6,3},{7,2},{8,13},{9,12},{10,... | collective-permute-start | bytes 12296 | tf_op jit(solution)/shard_map/ppermute | solution.py:83
  51.0 6.5 %collective-permute-start.5 = (bf16[2,1,1024]{2,0,1:T(2,128)(2,1)S(1)}, bf16[2,1,1024]{2,0,1:T(2,128)(2,1)S(1)}, u32[]{:S(2)}, u32[]{:S(2)}) collective-permute-start(bf16[2,1,1024]{2,0,1:T(2,128)(2,1)S(1)} %get-tuple-element.11), channel_id=1, source_target_pairs={{0,6},{1,7},{2,4},{3,5},{4,2},{5,3},{6,0},{7,1},{8,14},{9,15},{10,... | collective-permute-start | bytes 12296 | tf_op jit(solution)/shard_map/ppermute | solution.py:83
  51.6 8.8 %collective-permute-start.6 = (bf16[2,1,1024]{2,0,1:T(2,128)(2,1)S(1)}, bf16[2,1,1024]{2,0,1:T(2,128)(2,1)S(1)}, u32[]{:S(2)}, u32[]{:S(2)}) collective-permute-start(bf16[2,1,1024]{2,0,1:T(2,128)(2,1)S(1)} %get-tuple-element.10), channel_id=1, source_target_pairs={{0,7},{1,6},{2,5},{3,4},{4,3},{5,2},{6,1},{7,0},{8,15},{9,14},{10,... | collective-permute-start | bytes 12296 | tf_op jit(solution)/shard_map/ppermute | solution.py:83
  53.9 7.4 %collective-permute-start.7 = (bf16[2,1,1024]{2,0,1:T(2,128)(2,1)S(1)}, bf16[2,1,1024]{2,0,1:T(2,128)(2,1)S(1)}, u32[]{:S(2)}, u32[]{:S(2)}) collective-permute-start(bf16[2,1,1024]{2,0,1:T(2,128)(2,1)S(1)} %get-tuple-element.9), channel_id=1, source_target_pairs={{0,8},{1,9},{2,10},{3,11},{4,12},{5,13},{6,14},{7,15},{8,0},{9,1},... | collective-permute-start | bytes 12296 | tf_op jit(solution)/shard_map/ppermute | solution.py:83
  54.5 9.5 %collective-permute-start.8 = (bf16[2,1,1024]{2,0,1:T(2,128)(2,1)S(1)}, bf16[2,1,1024]{2,0,1:T(2,128)(2,1)S(1)}, u32[]{:S(2)}, u32[]{:S(2)}) collective-permute-start(bf16[2,1,1024]{2,0,1:T(2,128)(2,1)S(1)} %get-tuple-element.8), channel_id=1, source_target_pairs={{0,9},{1,8},{2,11},{3,10},{4,13},{5,12},{6,15},{7,14},{8,1},{9,0},... | collective-permute-start | bytes 12296 | tf_op jit(solution)/shard_map/ppermute | solution.py:83
  56.6 9.3 %collective-permute-start.9 = (bf16[2,1,1024]{2,0,1:T(2,128)(2,1)S(1)}, bf16[2,1,1024]{2,0,1:T(2,128)(2,1)S(1)}, u32[]{:S(2)}, u32[]{:S(2)}) collective-permute-start(bf16[2,1,1024]{2,0,1:T(2,128)(2,1)S(1)} %get-tuple-element.7), channel_id=1, source_target_pairs={{0,10},{1,11},{2,8},{3,9},{4,14},{5,15},{6,12},{7,13},{8,2},{9,3},... | collective-permute-start | bytes 12296 | tf_op jit(solution)/shard_map/ppermute | solution.py:83
  57.5 11.2 %collective-permute-start.10 = (bf16[2,1,1024]{2,0,1:T(2,128)(2,1)S(1)}, bf16[2,1,1024]{2,0,1:T(2,128)(2,1)S(1)}, u32[]{:S(2)}, u32[]{:S(2)}) collective-permute-start(bf16[2,1,1024]{2,0,1:T(2,128)(2,1)S(1)} %get-tuple-element.6), channel_id=1, source_target_pairs={{0,11},{1,10},{2,9},{3,8},{4,15},{5,14},{6,13},{7,12},{8,3},{9,2},... | collective-permute-start | bytes 12296 | tf_op jit(solution)/shard_map/ppermute | solution.py:83
  60.4 8.3 %collective-permute-start.11 = (bf16[2,1,1024]{2,0,1:T(2,128)(2,1)S(1)}, bf16[2,1,1024]{2,0,1:T(2,128)(2,1)S(1)}, u32[]{:S(2)}, u32[]{:S(2)}) collective-permute-start(bf16[2,1,1024]{2,0,1:T(2,128)(2,1)S(1)} %get-tuple-element.5), channel_id=1, source_target_pairs={{0,12},{1,13},{2,14},{3,15},{4,8},{5,9},{6,10},{7,11},{8,4},{9,5},... | collective-permute-start | bytes 12296 | tf_op jit(solution)/shard_map/ppermute | solution.py:83
  61.2 7.5 %collective-permute-start.12 = (bf16[2,1,1024]{2,0,1:T(2,128)(2,1)S(1)}, bf16[2,1,1024]{2,0,1:T(2,128)(2,1)S(1)}, u32[]{:S(2)}, u32[]{:S(2)}) collective-permute-start(bf16[2,1,1024]{2,0,1:T(2,128)(2,1)S(1)} %get-tuple-element.4), channel_id=1, source_target_pairs={{0,13},{1,12},{2,15},{3,14},{4,9},{5,8},{6,11},{7,10},{8,5},{9,4},... | collective-permute-start | bytes 12296 | tf_op jit(solution)/shard_map/ppermute | solution.py:83
  64.0 6.6 %collective-permute-start.13 = (bf16[2,1,1024]{2,0,1:T(2,128)(2,1)S(1)}, bf16[2,1,1024]{2,0,1:T(2,128)(2,1)S(1)}, u32[]{:S(2)}, u32[]{:S(2)}) collective-permute-start(bf16[2,1,1024]{2,0,1:T(2,128)(2,1)S(1)} %get-tuple-element.3), channel_id=1, source_target_pairs={{0,14},{1,15},{2,12},{3,13},{4,10},{5,11},{6,8},{7,9},{8,6},{9,7},... | collective-permute-start | bytes 12296 | tf_op jit(solution)/shard_map/ppermute | solution.py:83
  65.9 6.0 %collective-permute-start.14 = (bf16[2,1,1024]{2,0,1:T(2,128)(2,1)S(1)}, bf16[2,1,1024]{2,0,1:T(2,128)(2,1)S(1)}, u32[]{:S(2)}, u32[]{:S(2)}) collective-permute-start(bf16[2,1,1024]{2,0,1:T(2,128)(2,1)S(1)} %get-tuple-element.2), channel_id=1, source_target_pairs={{0,15},{1,14},{2,13},{3,12},{4,11},{5,10},{6,9},{7,8},{8,7},{9,6},... | collective-permute-start | bytes 12296 | tf_op jit(solution)/shard_map/ppermute | solution.py:83
  92.9 2.1 %copy-start.3 = (bf16[2,8,2048]{2,1,0:T(8,128)(2,1)}, bf16[2,8,2048]{2,1,0:T(8,128)(2,1)S(1)}, u32[]{:S(2)}) copy-start(bf16[2,8,2048]{2,1,0:T(8,128)(2,1)S(1)} %get-tuple-element.21) | copy-start | bytes 196612
  97.2 24.5 %copy-start.2 = (bf16[2,2048,384]{2,1,0:T(8,128)(2,1)S(1)}, bf16[2,2048,384]{2,1,0:T(8,128)(2,1)}, u32[]{:S(2)}) copy-start(bf16[2,2048,384]{2,1,0:T(8,128)(2,1)} %param.23) | copy-start | bytes 9437188
  120.8 0.9 copy-start.1
  126.8 6.9 %copy-start.4 = (f32[2,8,8]{2,1,0:T(8,128)S(1)}, f32[2,8,8]{2,1,0:T(8,128)}, u32[]{:S(2)}) copy-start(f32[2,8,8]{2,1,0:T(8,128)} %param.22) | copy-start | bytes 1540
  129.4 20.9 %all-to-all-start.4 = ((bf16[2,16,5,2048]{3,0,2,1:T(2,128)(2,1)}), bf16[2,16,5,2048]{3,0,2,1:T(2,128)(2,1)}, u32[]{:S(2)}, u32[]{:S(2)}) async-start(bf16[2,16,5,2048]{3,0,2,1:T(2,128)(2,1)} %bitcast.179), calls=%async_computation.4 | async-start | bytes 1310720 | tf_op jit(solution)/shard_map/all_to_all | solution.py:126
Sparse Core Ops, SparseCore 0:
  10.1 78.0 all-gather.1
